TPU v7x, 32 devices: a whole 2x2x4 slice. The times are simulated.
32 devices in a mesh: ctx: 16 (over z, y, x), head: 2 (over core).
Axes of the slice: x: 2, y: 2, z: 4, core: 2. Of those that a mesh axis runs over, the one named last changes fastest.
Arguments:
- queries: bfloat16 [8192, 4, 4, 128], P('ctx', 'head')
- keys: bfloat16 [8192, 4, 128], P('ctx')
- values: bfloat16 [8192, 4, 128], P('ctx'), may hold values from -6 to 6
- output_gradient: bfloat16 [8192, 4, 4, 128], P('ctx', 'head'), may hold values from -6 to 6
- selected: int32 [16, 2], replicated, may hold values from 0 to 14, as said below
Outputs:
- attn_out: bfloat16 [8192, 4, 4, 128], P('ctx', 'head')
- grad_q: bfloat16 [8192, 4, 4, 128], P('ctx', 'head')
- grad_k: bfloat16 [8192, 4, 128], P('ctx', 'head')
- grad_v: bfloat16 [8192, 4, 128], P('ctx', 'head')
Inputs may be any that keep to these rules, and one draw needn't show every extreme that they name: selected[b, j] <= b for every block b; an entry equal to b selects no block; for b >= 2 the two entries of a row differ and both are below b.
All inputs are finite; a program needn't handle non-finite values.
Results may differ from a plain program's by a relative error of at most 0.011.
Values may be sent and summed in bfloat16 or wider, within the bound.
A program may use at most 128 MiB of HBM per device.

v0:
```python
import jax
import jax.numpy as jnp
from jax import lax
from jax.sharding import PartitionSpec as P


def fetch_blocks(own_keys, own_values, selected, piece_rows):
    held_keys, held_values = (
        lax.all_to_all(own_keys, "ctx", split_axis=0, concat_axis=0, tiled=True),
        lax.all_to_all(own_values, "ctx", split_axis=0, concat_axis=0, tiled=True),
    )
    blocks = selected.shape[0]
    layout = (blocks, piece_rows) + own_keys.shape[1:]
    wanted = jnp.transpose(selected)
    send_keys = held_keys.reshape(layout)[wanted]
    send_values = held_values.reshape(layout)[wanted]
    got_keys, got_values = (
        lax.all_to_all(send_keys, "ctx", split_axis=1, concat_axis=1, tiled=True),
        lax.all_to_all(send_values, "ctx", split_axis=1, concat_axis=1, tiled=True),
    )
    joined = (2, blocks * piece_rows) + own_keys.shape[1:]
    return (got_keys.reshape(joined), got_values.reshape(joined))


def return_home(part_keys, part_values, selected, piece_rows):
    blocks = selected.shape[0]
    rows_block = blocks * piece_rows
    trailing = part_keys.shape[1:]
    layout = (2, blocks, piece_rows) + trailing
    back_keys, back_values = (
        lax.all_to_all(
            part_keys[: 2 * rows_block].reshape(layout),
            "ctx",
            split_axis=1,
            concat_axis=1,
            tiled=True,
        ),
        lax.all_to_all(
            part_values[: 2 * rows_block].reshape(layout),
            "ctx",
            split_axis=1,
            concat_axis=1,
            tiled=True,
        ),
    )
    owners = (
        jnp.transpose(selected)[:, :, None] == jnp.arange(blocks, dtype=jnp.int32)[None, None, :]
    ).astype(jnp.float32)

    def collect(arrived):
        summed = jnp.einsum(
            "jrb,jrx->bx", owners, arrived.reshape(2, blocks, -1), precision=lax.Precision.HIGHEST
        )
        return summed.reshape((blocks, piece_rows) + trailing)

    home_keys, home_values = (
        lax.all_to_all(collect(back_keys), "ctx", split_axis=0, concat_axis=0, tiled=True),
        lax.all_to_all(collect(back_values), "ctx", split_axis=0, concat_axis=0, tiled=True),
    )
    own_rows = (rows_block,) + trailing
    return (
        home_keys.reshape(own_rows) + part_keys[2 * rows_block :],
        home_values.reshape(own_rows) + part_values[2 * rows_block :],
    )


def attend_head(queries_head, keys_head, values_head, grads_head, visible, softmax_scale):
    scores = (
        jnp.einsum("qgd,kd->gqk", queries_head, keys_head, preferred_element_type=jnp.float32)
        * softmax_scale
    )
    scores = jnp.where(visible[None], scores, -jnp.inf)
    row_max = jnp.max(scores, axis=-1, keepdims=True)
    weights = jnp.exp(scores - row_max)
    probs = weights / jnp.sum(weights, axis=-1, keepdims=True)
    probs_low = probs.astype(jnp.bfloat16)
    head_out = jnp.einsum(
        "gqk,kd->qgd", probs_low, values_head, preferred_element_type=jnp.float32
    ).astype(jnp.bfloat16)
    row_dot = jnp.sum(grads_head.astype(jnp.float32) * head_out.astype(jnp.float32), axis=-1)
    grad_probs = jnp.einsum(
        "qgd,kd->gqk", grads_head, values_head, preferred_element_type=jnp.float32
    )
    grad_scores = (
        probs * (grad_probs - jnp.transpose(row_dot)[:, :, None]) * softmax_scale
    ).astype(jnp.bfloat16)
    head_dq = jnp.einsum(
        "gqk,kd->qgd", grad_scores, keys_head, preferred_element_type=jnp.float32
    ).astype(jnp.bfloat16)
    head_dk = jnp.einsum(
        "gqk,qgd->kd", grad_scores, queries_head, preferred_element_type=jnp.float32
    )
    head_dv = jnp.einsum("gqk,qgd->kd", probs_low, grads_head, preferred_element_type=jnp.float32)
    return (head_out, head_dq, head_dk, head_dv)


def on_device(queries, keys, values, output_gradient, selected):
    rows_block = queries.shape[0]
    kv_count = keys.shape[1]
    head_size = keys.shape[2]
    piece_rows = rows_block // lax.axis_size("ctx")
    own_index = lax.axis_index("ctx")
    softmax_scale = head_size ** (-0.5)
    near_keys, near_values = fetch_blocks(keys, values, selected, piece_rows)
    all_keys = jnp.concatenate([near_keys[0], near_keys[1], keys], axis=0)
    all_values = jnp.concatenate([near_values[0], near_values[1], values], axis=0)
    own_picks = lax.dynamic_index_in_dim(selected, own_index, 0, keepdims=False)
    position = jnp.arange(rows_block, dtype=jnp.int32)
    causal = position[:, None] >= position[None, :]
    visible = jnp.concatenate(
        [
            jnp.broadcast_to(own_picks[0] < own_index, (rows_block, rows_block)),
            jnp.broadcast_to(own_picks[1] < own_index, (rows_block, rows_block)),
            causal,
        ],
        axis=1,
    )

    def per_head(head_pos, totals):
        attn_acc, dq_acc, dk_acc, dv_acc = totals
        head_out, head_dq, head_dk, head_dv = attend_head(
            lax.dynamic_index_in_dim(queries, head_pos, 2, keepdims=False),
            lax.dynamic_index_in_dim(all_keys, head_pos, 1, keepdims=False),
            lax.dynamic_index_in_dim(all_values, head_pos, 1, keepdims=False),
            lax.dynamic_index_in_dim(output_gradient, head_pos, 2, keepdims=False),
            visible,
            softmax_scale,
        )
        attn_acc = lax.dynamic_update_index_in_dim(attn_acc, head_out, head_pos, 2)
        dq_acc = lax.dynamic_update_index_in_dim(dq_acc, head_dq, head_pos, 2)
        dk_acc = lax.dynamic_update_index_in_dim(dk_acc, head_dk, head_pos, 1)
        dv_acc = lax.dynamic_update_index_in_dim(dv_acc, head_dv, head_pos, 1)
        return (attn_acc, dq_acc, dk_acc, dv_acc)

    initial = (
        jnp.zeros(queries.shape, jnp.bfloat16),
        jnp.zeros(queries.shape, jnp.bfloat16),
        jnp.zeros(all_keys.shape, jnp.float32),
        jnp.zeros(all_keys.shape, jnp.float32),
    )
    attn_out, grad_q, part_keys, part_values = lax.fori_loop(0, kv_count, per_head, initial)
    grad_keys, grad_values = return_home(part_keys, part_values, selected, piece_rows)
    grad_keys, grad_values = (
        lax.psum_scatter(grad_keys, "head", scatter_dimension=1, tiled=True),
        lax.psum_scatter(grad_values, "head", scatter_dimension=1, tiled=True),
    )
    return (attn_out, grad_q, grad_keys.astype(jnp.bfloat16), grad_values.astype(jnp.bfloat16))


def solution(mesh):
    return jax.shard_map(
        on_device,
        mesh=mesh,
        in_specs=(
            P("ctx", "head", None, None),
            P("ctx", None, None),
            P("ctx", None, None),
            P("ctx", "head", None, None),
            P(),
        ),
        out_specs=(
            P("ctx", "head", None, None),
            P("ctx", "head", None, None),
            P("ctx", "head", None),
            P("ctx", "head", None),
        ),
        check_vma=False,
    )
```

profile of v0, /device:TPU:0, one launch (start us, length us, event | category | flops | bytes accessed | tf_op | source)
XLA Modules:
  0.0 373.0 jit_solution(18032600717242512195)
XLA Ops:
  7.2 23.4 %all_to_all.40 = bf16[512,4,128]{2,1,0:T(4,128)(2,1)S(1)} all-to-all(bf16[512,4,128]{2,1,0:T(4,128)(2,1)} %param.9), channel_id=1, replica_groups=mesh['ctx'=16,'head'=2] {'ctx'}, dimensions={0} | all-to-all | bytes 1048576 | tf_op jit(solution)/shard_map/all_to_all | solution.py:10
  30.6 3.9 %all-to-all-start.2 = ((bf16[512,4,128]{2,1,0:T(4,128)(2,1)}), bf16[512,4,128]{2,1,0:T(4,128)(2,1)S(1)}, u32[]{:S(2)}, u32[]{:S(2)}) async-start(bf16[512,4,128]{2,1,0:T(4,128)(2,1)} %param.8), calls=%async_computation.2 | async-start | bytes 1048576 | tf_op jit(solution)/shard_map/all_to_all | solution.py:9
  37.3 11.7 %all-to-all-done.2 = bf16[512,4,128]{2,1,0:T(4,128)(2,1)S(1)} async-done(((bf16[512,4,128]{2,1,0:T(4,128)(2,1)}), bf16[512,4,128]{2,1,0:T(4,128)(2,1)S(1)}, u32[]{:S(2)}, u32[]{:S(2)}) %all-to-all-start.2) | async-done | bytes 524320 | tf_op jit(solution)/shard_map/all_to_all | solution.py:9
  49.0 3.9 %all-to-all-start.1 = ((bf16[2,16,32,4,128]{4,2,3,0,1:T(8,128)(2,1)}), bf16[2,16,32,4,128]{4,2,3,0,1:T(8,128)(2,1)S(1)}, u32[]{:S(2)}, u32[]{:S(2)}) async-start(bf16[2,16,32,4,128]{4,2,3,0,1:T(8,128)(2,1)} %copy.141), calls=%async_computation.1 | async-start | bytes 2097152 | tf_op jit(solution)/shard_map/all_to_all | solution.py:19
  54.8 21.7 %all-to-all-done.1 = bf16[2,16,32,4,128]{4,2,3,0,1:T(8,128)(2,1)S(1)} async-done(((bf16[2,16,32,4,128]{4,2,3,0,1:T(8,128)(2,1)}), bf16[2,16,32,4,128]{4,2,3,0,1:T(8,128)(2,1)S(1)}, u32[]{:S(2)}, u32[]{:S(2)}) %all-to-all-start.1) | async-done | bytes 1048608 | tf_op jit(solution)/shard_map/all_to_all | solution.py:19
  76.5 5.9 %all-to-all-start.3 = ((bf16[2,16,32,4,128]{4,2,3,0,1:T(8,128)(2,1)}), bf16[2,16,32,4,128]{4,2,3,0,1:T(8,128)(2,1)S(1)}, u32[]{:S(2)}, u32[]{:S(2)}) async-start(bf16[2,16,32,4,128]{4,2,3,0,1:T(8,128)(2,1)} %copy.147), calls=%async_computation.3 | async-start | bytes 2097152 | tf_op jit(solution)/shard_map/all_to_all | solution.py:18
  94.2 11.1 %all-to-all-done.3 = bf16[2,16,32,4,128]{4,2,3,0,1:T(8,128)(2,1)S(1)} async-done(((bf16[2,16,32,4,128]{4,2,3,0,1:T(8,128)(2,1)}), bf16[2,16,32,4,128]{4,2,3,0,1:T(8,128)(2,1)S(1)}, u32[]{:S(2)}, u32[]{:S(2)}) %all-to-all-start.3) | async-done | bytes 1048608 | tf_op jit(solution)/shard_map/all_to_all | solution.py:18
  108.9 75.0 %while.19 = (s32[]{:T(128)}, bf16[512,2,4,128]{0,3,1,2:T(8,128)(2,1)}, bf16[512,2,4,128]{0,3,1,2:T(8,128)(2,1)}, f32[1536,4,128]{2,0,1:T(8,128)}, f32[1536,4,128...) while((s32[]{:T(128)}, ...), condition=%wide.region_4.5_spmd, body=%wide.region_0.4_spmd.sunk | while | flops 2434007552 | bytes 79718664 | solution.py:141
  108.9 6.1 %fusion.107 = (f32[2,512]{1,0:T(2,128)S(1)}, f32[2,512,1536]{1,2,0:T(8,128)}) fusion(pred[512,1536]{0,1:T(8,128)(4,1)S(1)} %get-tuple-element.393, bf16[1536,4,128]{2,0,1:T(8,128)(2,1)} %get-tuple-element.394, s32[]{:T(128)} %get-tuple-element.376, bf16[512,2,4,128]{3,0,1,2:T(8,128)(2,1)} %get-tuple-element.395), kind=kOutput, calls=%fused_computation.78.clone.1 | convolution fusion | flops 408946176 | bytes 7738368 | tf_op jit(solution)/shard_map/while/body/eval_jaxpr/sub | solution.py:74
  115.1 3.9 %fusion.108 = bf16[2,512,1536]{1,2,0:T(8,128)(2,1)S(1)} fusion(f32[2,512,1536]{1,2,0:T(8,128)} %get-tuple-element.361, f32[2,512]{1,0:T(2,128)S(1)} %get-tuple-element.362), kind=kLoop, calls=%fused_computation.14.clone.1 | loop fusion | flops 3145728 | bytes 9441280 | tf_op jit(solution)/shard_map/while/body/eval_jaxpr/convert_element_type | solution.py:76
  127.6 6.1 %fusion.107 = (f32[2,512]{1,0:T(2,128)S(1)}, f32[2,512,1536]{1,2,0:T(8,128)}) fusion(pred[512,1536]{0,1:T(8,128)(4,1)S(1)} %get-tuple-element.393, bf16[1536,4,128]{2,0,1:T(8,128)(2,1)} %get-tuple-element.394, s32[]{:T(128)} %get-tuple-element.376, bf16[512,2,4,128]{3,0,1,2:T(8,128)(2,1)} %get-tuple-element.395), kind=kOutput, calls=%fused_computation.78.clone.1 | convolution fusion | flops 408946176 | bytes 7738368 | tf_op jit(solution)/shard_map/while/body/eval_jaxpr/sub | solution.py:74
  146.4 6.1 %fusion.107 = (f32[2,512]{1,0:T(2,128)S(1)}, f32[2,512,1536]{1,2,0:T(8,128)}) fusion(pred[512,1536]{0,1:T(8,128)(4,1)S(1)} %get-tuple-element.393, bf16[1536,4,128]{2,0,1:T(8,128)(2,1)} %get-tuple-element.394, s32[]{:T(128)} %get-tuple-element.376, bf16[512,2,4,128]{3,0,1,2:T(8,128)(2,1)} %get-tuple-element.395), kind=kOutput, calls=%fused_computation.78.clone.1 | convolution fusion | flops 408946176 | bytes 7738368 | tf_op jit(solution)/shard_map/while/body/eval_jaxpr/sub | solution.py:74
  165.1 6.1 %fusion.107 = (f32[2,512]{1,0:T(2,128)S(1)}, f32[2,512,1536]{1,2,0:T(8,128)}) fusion(pred[512,1536]{0,1:T(8,128)(4,1)S(1)} %get-tuple-element.393, bf16[1536,4,128]{2,0,1:T(8,128)(2,1)} %get-tuple-element.394, s32[]{:T(128)} %get-tuple-element.376, bf16[512,2,4,128]{3,0,1,2:T(8,128)(2,1)} %get-tuple-element.395), kind=kOutput, calls=%fused_computation.78.clone.1 | convolution fusion | flops 408946176 | bytes 7738368 | tf_op jit(solution)/shard_map/while/body/eval_jaxpr/sub | solution.py:74
  188.7 6.0 %all-to-all-start.6 = ((f32[2,16,32,4,128]{4,3,2,0,1:T(4,128)}), f32[2,16,32,4,128]{4,3,2,0,1:T(4,128)S(1)}, u32[]{:S(2)}, u32[]{:S(2)}) async-start(f32[2,16,32,4,128]{4,3,2,0,1:T(4,128)} %copy.159), calls=%async_computation.7 | async-start | bytes 4194304 | tf_op jit(solution)/shard_map/all_to_all | solution.py:38
  199.6 36.9 %all-to-all-done.6 = f32[2,16,32,4,128]{4,3,2,0,1:T(4,128)S(1)} async-done(((f32[2,16,32,4,128]{4,3,2,0,1:T(4,128)}), f32[2,16,32,4,128]{4,3,2,0,1:T(4,128)S(1)}, u32[]{:S(2)}, u32[]{:S(2)}) %all-to-all-start.6) | async-done | bytes 2097184 | tf_op jit(solution)/shard_map/all_to_all | solution.py:38
  237.9 9.8 %all-to-all-start.4 = ((f32[2,16,32,4,128]{4,3,2,0,1:T(4,128)}), f32[2,16,32,4,128]{4,3,2,0,1:T(4,128)S(1)}, u32[]{:S(2)}, u32[]{:S(2)}) async-start(f32[2,16,32,4,128]{4,3,2,0,1:T(4,128)} %copy.154), calls=%async_computation.4 | async-start | bytes 4194304 | tf_op jit(solution)/shard_map/all_to_all | solution.py:31
  247.7 3.9 %reshape.93 = f32[2,16,16384]{2,0,1:T(2,128)} reshape(f32[2,16,32,4,128]{4,3,2,0,1:T(4,128)} %copy-done) | data formatting | bytes 4194304 | tf_op jit(solution)/shard_map/reshape | solution.py:52
  251.6 4.2 %copy.200 = f32[2,16,16384]{2,1,0:T(8,128)} copy(f32[2,16,16384]{2,0,1:T(2,128)} %reshape.93) | data formatting | bytes 4194304 | tf_op jit(solution)/shard_map/reshape | solution.py:52
  264.3 25.9 %all-to-all-done.4 = f32[2,16,32,4,128]{4,3,2,0,1:T(4,128)S(1)} async-done(((f32[2,16,32,4,128]{4,3,2,0,1:T(4,128)}), f32[2,16,32,4,128]{4,3,2,0,1:T(4,128)S(1)}, u32[]{:S(2)}, u32[]{:S(2)}) %all-to-all-start.4) | async-done | bytes 2097184 | tf_op jit(solution)/shard_map/all_to_all | solution.py:31
  290.2 9.8 %all-to-all-start.7 = ((f32[16,32,4,128]{3,2,1,0:T(4,128)}), f32[16,32,4,128]{3,2,1,0:T(4,128)S(1)}, u32[]{:S(2)}, u32[]{:S(2)}) async-start(f32[16,32,4,128]{3,2,1,0:T(4,128)} %copy.162), calls=%async_computation.8 | async-start | bytes 2097152 | tf_op jit(solution)/shard_map/all_to_all | solution.py:58
  312.8 10.9 %all-to-all-done.7 = f32[16,32,4,128]{3,2,1,0:T(4,128)S(1)} async-done(((f32[16,32,4,128]{3,2,1,0:T(4,128)}), f32[16,32,4,128]{3,2,1,0:T(4,128)S(1)}, u32[]{:S(2)}, u32[]{:S(2)}) %all-to-all-start.7) | async-done | bytes 1048608 | tf_op jit(solution)/shard_map/all_to_all | solution.py:58
  323.7 5.9 %all-to-all-start.5 = ((f32[16,32,4,128]{3,2,1,0:T(4,128)}), f32[16,32,4,128]{3,2,1,0:T(4,128)S(1)}, u32[]{:S(2)}, u32[]{:S(2)}) async-start(f32[16,32,4,128]{3,2,1,0:T(4,128)} %copy.157), calls=%async_computation.5 | async-start | bytes 2097152 | tf_op jit(solution)/shard_map/all_to_all | solution.py:57
  332.2 20.3 %all-to-all-done.5 = f32[16,32,4,128]{3,2,1,0:T(4,128)S(1)} async-done(((f32[16,32,4,128]{3,2,1,0:T(4,128)}), f32[16,32,4,128]{3,2,1,0:T(4,128)S(1)}, u32[]{:S(2)}, u32[]{:S(2)}) %all-to-all-start.5) | async-done | bytes 1048608 | tf_op jit(solution)/shard_map/all_to_all | solution.py:57
  360.1 3.9 %reduce-scatter.3.cloned.1.call-done = f32[512,2,128]{2,0,1:T(8,128)} async-done(((f32[512,4,128]{2,0,1:T(8,128)}), f32[512,2,128]{2,0,1:T(8,128)}) %reduce-scatter.3.cloned.1.call-update) | async-done | bytes 524304 | tf_op jit(solution)/shard_map/reduce_scatter | solution.py:144
  (155 shorter events, 109.6 us)
Async XLA Ops:
  30.6 18.4 %all-to-all-start.2 = ((bf16[512,4,128]{2,1,0:T(4,128)(2,1)}), bf16[512,4,128]{2,1,0:T(4,128)(2,1)S(1)}, u32[]{:S(2)}, u32[]{:S(2)}) async-start(bf16[512,4,128]{2,1,0:T(4,128)(2,1)} %param.8), calls=%async_computation.2 | async-start | bytes 1048576 | tf_op jit(solution)/shard_map/all_to_all | solution.py:9
  49.0 27.5 %all-to-all-start.1 = ((bf16[2,16,32,4,128]{4,2,3,0,1:T(8,128)(2,1)}), bf16[2,16,32,4,128]{4,2,3,0,1:T(8,128)(2,1)S(1)}, u32[]{:S(2)}, u32[]{:S(2)}) async-start(bf16[2,16,32,4,128]{4,2,3,0,1:T(8,128)(2,1)} %copy.141), calls=%async_computation.1 | async-start | bytes 2097152 | tf_op jit(solution)/shard_map/all_to_all | solution.py:19
  53.0 29.4 %copy-start.3 = (bf16[512,4,128]{2,1,0:T(4,128)(2,1)S(1)}, bf16[512,4,128]{2,1,0:T(4,128)(2,1)}, u32[]{:S(2)}) copy-start(bf16[512,4,128]{2,1,0:T(4,128)(2,1)} %param.9) | copy-start | bytes 1572868
  53.8 29.5 %copy-start.4 = (bf16[512,4,128]{2,1,0:T(4,128)(2,1)S(1)}, bf16[512,4,128]{2,1,0:T(4,128)(2,1)}, u32[]{:S(2)}) copy-start(bf16[512,4,128]{2,1,0:T(4,128)(2,1)} %param.8) | copy-start | bytes 1572868
  53.8 30.4 %copy-start.12 = (s32[16,2]{0,1:T(2,128)S(1)}, s32[16,2]{0,1:T(2,128)}, u32[]{:S(2)}) copy-start(s32[16,2]{0,1:T(2,128)} %param.11) | copy-start | bytes 388
  76.5 28.8 %all-to-all-start.3 = ((bf16[2,16,32,4,128]{4,2,3,0,1:T(8,128)(2,1)}), bf16[2,16,32,4,128]{4,2,3,0,1:T(8,128)(2,1)S(1)}, u32[]{:S(2)}, u32[]{:S(2)}) async-start(bf16[2,16,32,4,128]{4,2,3,0,1:T(8,128)(2,1)} %copy.147), calls=%async_computation.3 | async-start | bytes 2097152 | tf_op jit(solution)/shard_map/all_to_all | solution.py:18
  115.0 4.6 %slice-start = ((s8[6291456]{0:T(1024)(128)(4,1)}), s8[4194304]{0:T(1024)(128)(4,1)S(1)}, s32[]{:S(2)}) async-start(s8[6291456]{0:T(1024)(128)(4,1)} %bitcast.170), calls=%async_computation.12 | async-start | bytes 8388608 | tf_op jit(solution)/shard_map/while
  115.0 3.9 %copy-start.5 = (bf16[512,2,4,128]{0,3,1,2:T(8,128)(2,1)S(1)}, bf16[512,2,4,128]{0,3,1,2:T(8,128)(2,1)}, u32[]{:S(2)}) copy-start(bf16[512,2,4,128]{0,3,1,2:T(8,128)(2,1)} %get-tuple-element.377) | copy-start | bytes 3145732 | tf_op jit(solution)/shard_map/while
  115.0 5.0 %slice-start.1 = ((s8[6291456]{0:T(1024)(128)(4,1)}), s8[2097152]{0:T(1024)(128)(4,1)S(1)}, s32[]{:S(2)}) async-start(s8[6291456]{0:T(1024)(128)(4,1)} %bitcast.170), calls=%async_computation.13 | async-start | bytes 4194304 | tf_op jit(solution)/shard_map/while
  133.8 4.6 %slice-start = ((s8[6291456]{0:T(1024)(128)(4,1)}), s8[4194304]{0:T(1024)(128)(4,1)S(1)}, s32[]{:S(2)}) async-start(s8[6291456]{0:T(1024)(128)(4,1)} %bitcast.170), calls=%async_computation.12 | async-start | bytes 8388608 | tf_op jit(solution)/shard_map/while
  133.8 3.9 %copy-start.5 = (bf16[512,2,4,128]{0,3,1,2:T(8,128)(2,1)S(1)}, bf16[512,2,4,128]{0,3,1,2:T(8,128)(2,1)}, u32[]{:S(2)}) copy-start(bf16[512,2,4,128]{0,3,1,2:T(8,128)(2,1)} %get-tuple-element.377) | copy-start | bytes 3145732 | tf_op jit(solution)/shard_map/while
  133.8 5.0 %slice-start.1 = ((s8[6291456]{0:T(1024)(128)(4,1)}), s8[2097152]{0:T(1024)(128)(4,1)S(1)}, s32[]{:S(2)}) async-start(s8[6291456]{0:T(1024)(128)(4,1)} %bitcast.170), calls=%async_computation.13 | async-start | bytes 4194304 | tf_op jit(solution)/shard_map/while
  152.5 4.6 %slice-start = ((s8[6291456]{0:T(1024)(128)(4,1)}), s8[4194304]{0:T(1024)(128)(4,1)S(1)}, s32[]{:S(2)}) async-start(s8[6291456]{0:T(1024)(128)(4,1)} %bitcast.170), calls=%async_computation.12 | async-start | bytes 8388608 | tf_op jit(solution)/shard_map/while
  152.5 5.0 %slice-start.1 = ((s8[6291456]{0:T(1024)(128)(4,1)}), s8[2097152]{0:T(1024)(128)(4,1)S(1)}, s32[]{:S(2)}) async-start(s8[6291456]{0:T(1024)(128)(4,1)} %bitcast.170), calls=%async_computation.13 | async-start | bytes 4194304 | tf_op jit(solution)/shard_map/while
  171.3 4.6 %slice-start = ((s8[6291456]{0:T(1024)(128)(4,1)}), s8[4194304]{0:T(1024)(128)(4,1)S(1)}, s32[]{:S(2)}) async-start(s8[6291456]{0:T(1024)(128)(4,1)} %bitcast.170), calls=%async_computation.12 | async-start | bytes 8388608 | tf_op jit(solution)/shard_map/while
  171.3 5.0 %slice-start.1 = ((s8[6291456]{0:T(1024)(128)(4,1)}), s8[2097152]{0:T(1024)(128)(4,1)S(1)}, s32[]{:S(2)}) async-start(s8[6291456]{0:T(1024)(128)(4,1)} %bitcast.170), calls=%async_computation.13 | async-start | bytes 4194304 | tf_op jit(solution)/shard_map/while
  188.7 47.8 %all-to-all-start.6 = ((f32[2,16,32,4,128]{4,3,2,0,1:T(4,128)}), f32[2,16,32,4,128]{4,3,2,0,1:T(4,128)S(1)}, u32[]{:S(2)}, u32[]{:S(2)}) async-start(f32[2,16,32,4,128]{4,3,2,0,1:T(4,128)} %copy.159), calls=%async_computation.7 | async-start | bytes 4194304 | tf_op jit(solution)/shard_map/all_to_all | solution.py:38
  237.9 52.3 %all-to-all-start.4 = ((f32[2,16,32,4,128]{4,3,2,0,1:T(4,128)}), f32[2,16,32,4,128]{4,3,2,0,1:T(4,128)S(1)}, u32[]{:S(2)}, u32[]{:S(2)}) async-start(f32[2,16,32,4,128]{4,3,2,0,1:T(4,128)} %copy.154), calls=%async_computation.4 | async-start | bytes 4194304 | tf_op jit(solution)/shard_map/all_to_all | solution.py:31
  290.2 33.5 %all-to-all-start.7 = ((f32[16,32,4,128]{3,2,1,0:T(4,128)}), f32[16,32,4,128]{3,2,1,0:T(4,128)S(1)}, u32[]{:S(2)}, u32[]{:S(2)}) async-start(f32[16,32,4,128]{3,2,1,0:T(4,128)} %copy.162), calls=%async_computation.8 | async-start | bytes 2097152 | tf_op jit(solution)/shard_map/all_to_all | solution.py:58
  323.7 28.8 %all-to-all-start.5 = ((f32[16,32,4,128]{3,2,1,0:T(4,128)}), f32[16,32,4,128]{3,2,1,0:T(4,128)S(1)}, u32[]{:S(2)}, u32[]{:S(2)}) async-start(f32[16,32,4,128]{3,2,1,0:T(4,128)} %copy.157), calls=%async_computation.5 | async-start | bytes 2097152 | tf_op jit(solution)/shard_map/all_to_all | solution.py:57
  329.5 28.5 %reduce-scatter.5.cloned.1.call-start = ((), (), s32[]{:S(2)}) async-start(), calls=%async_computation.11 | async-start | bytes 1572864 | tf_op jit(solution)/shard_map/reduce_scatter | solution.py:145
  332.2 23.0 %copy-start.7 = (bf16[512,2,4,128]{0,3,1,2:T(8,128)(2,1)S(1)}, bf16[512,2,4,128]{0,3,1,2:T(8,128)(2,1)}, u32[]{:S(2)}) copy-start(bf16[512,2,4,128]{0,3,1,2:T(8,128)(2,1)} %get-tuple-element.260) | copy-start | bytes 3145732
  332.2 31.9 %reduce-scatter.3.cloned.1.call-start = ((), (), s32[]{:S(2)}) async-start(), calls=%async_computation.10 | async-start | bytes 1572864 | tf_op jit(solution)/shard_map/reduce_scatter | solution.py:144
  352.7 4.0 %copy-start.10 = (bf16[512,2,4,128]{0,3,1,2:T(8,128)(2,1)S(1)}, bf16[512,2,4,128]{0,3,1,2:T(8,128)(2,1)}, u32[]{:S(2)}) copy-start(bf16[512,2,4,128]{0,3,1,2:T(8,128)(2,1)} %get-tuple-element.261) | copy-start | bytes 3145732
  (18 other events, 39.7 us)
Sparse Core Ops, SparseCore 0:
  332.6 9.6 reduce-scatter.4
  355.2 8.7 reduce-scatter.2
where the time goes:
time: 375 us; the launch traced here: 373 us
  waiting for transfers between devices  142 us (38%)
  matrix products  64.4 us (17%)
  local copies, waits for them, and re-layouts  53.3 us (14%)
  starting transfers between devices  45.3 us (12%)
  other arithmetic  28.3 us (8%)
  blocking collectives  23.4 us (6%)
  between operations  15.6 us (4%)
    all_to_all x1, waiting for transfers between devices, return_home(): lax.all_to_all(part_values[:2 * rows_block].reshape(layout), 'ctx', split...  36.9 us
    all_to_all x1, waiting for transfers between devices, return_home(): lax.all_to_all(part_keys[:2 * rows_block].reshape(layout), 'ctx', split_a...  25.9 us
    sub x4, matrix products, attend_head(): weights = jnp.exp(scores - row_max)  24.5 us
    all_to_all x1, blocking collectives, fetch_blocks(): lax.all_to_all(own_values, 'ctx', split_axis=0, concat_axis=0, tiled=True)  23.4 us
    all_to_all x1, waiting for transfers between devices, fetch_blocks(): lax.all_to_all(send_values, 'ctx', split_axis=1, concat_axis=1, tiled=True)  21.7 us
    all_to_all x1, waiting for transfers between devices, return_home(): lax.all_to_all(collect(back_keys), 'ctx', split_axis=0, concat_axis=0, ti...  20.3 us
    convert_element_type x4, other arithmetic, attend_head(): probs_low = probs.astype(jnp.bfloat16)  15.5 us
    reshape x4, local copies, waits for them, and re-layouts, collect(): arrived.reshape(2, blocks, -1)  13.6 us
  transfers between devices with their start and end apart: 9, of which 8 were waited for; matrix products, arithmetic and copies ran while one was open for 16% of the time, Pallas kernels for 0%

commit v1 on v0

--- a/solution.py
+++ b/solution.py
@@ -2,6 +2,13 @@
 import jax.numpy as jnp
 from jax import lax
 from jax.sharding import PartitionSpec as P
+
+
+def stacked_exchange(x, axis, split, join):
+    size = lax.axis_size(axis)
+    tiles = jnp.stack(jnp.split(x, size, axis=split), axis=0)
+    tiles = lax.all_to_all(tiles, axis, split_axis=0, concat_axis=0)
+    return jnp.concatenate(tiles, axis=join)
 
 
 def fetch_blocks(own_keys, own_values, selected, piece_rows):
@@ -16,7 +23,7 @@
     send_values = held_values.reshape(layout)[wanted]
     got_keys, got_values = (
         lax.all_to_all(send_keys, "ctx", split_axis=1, concat_axis=1, tiled=True),
-        lax.all_to_all(send_values, "ctx", split_axis=1, concat_axis=1, tiled=True),
+        stacked_exchange(send_values, "ctx", 1, 1),
     )
     joined = (2, blocks * piece_rows) + own_keys.shape[1:]
     return (got_keys.reshape(joined), got_values.reshape(joined))

time: 375 us -> 375 us (level)
  blocking collectives: 23.4 us -> 0 us
  local copies, waits for them, and re-layouts: 53.3 us -> 62.5 us
  starting transfers between devices: 45.3 us -> 53.6 us
  waiting for transfers between devices: 142 us -> 148 us
    all_to_all x1 -> x0, blocking collectives: 23.4 us -> none  [fetch_blocks(): lax.all_to_all(own_values, 'ctx', split_axis=0, concat_axis=0, tiled=True)]
    all_to_all x1 -> x2, waiting for transfers between devices: 21.7 us -> 36 us  [the longest x1 21.7 us: stacked_exchange(): tiles = lax.all_to_all(tiles, axis, split_axis=0, concat_axis=0)]
    all_to_all x1 -> x2, starting transfers between devices: 3.88 us -> 12.2 us  [the longest x1 8.35 us: fetch_blocks(): lax.all_to_all(own_values, 'ctx', split_axis=0, concat_axis=0, tiled=True)]
    all_to_all x1, waiting for transfers between devices: 11.7 us -> 3.4 us  [fetch_blocks(): lax.all_to_all(own_keys, 'ctx', split_axis=0, concat_axis=0, tiled=True)]
    unnamed x28 -> x41, local copies, waits for them, and re-layouts: 10.9 us -> 18.6 us
  transfers between devices with their start and end apart: 9 -> 10, of which waited for: 8 -> 9; matrix products, arithmetic and copies ran while one was open for 16% -> 18% of each run, Pallas kernels for 0% -> 0%
where the time goes in v1:
time: 375 us; the launch traced here: 373 us
  waiting for transfers between devices  148 us (39%)
  matrix products  64.3 us (17%)
  local copies, waits for them, and re-layouts  62.5 us (17%)
  starting transfers between devices  53.6 us (14%)
  other arithmetic  28.3 us (8%)
  between operations  15.7 us (4%)
    all_to_all x1, waiting for transfers between devices, return_home(): lax.all_to_all(part_values[:2 * rows_block].reshape(layout), 'ctx', split...  36.9 us
    all_to_all x1, waiting for transfers between devices, return_home(): lax.all_to_all(part_keys[:2 * rows_block].reshape(layout), 'ctx', split_a...  25.9 us
    sub x4, matrix products, attend_head(): weights = jnp.exp(scores - row_max)  24.4 us
    all_to_all x1, waiting for transfers between devices, stacked_exchange(): tiles = lax.all_to_all(tiles, axis, split_axis=0, concat_axis=0)  21.7 us
    all_to_all x1, waiting for transfers between devices, return_home(): lax.all_to_all(collect(back_keys), 'ctx', split_axis=0, concat_axis=0, ti...  20.3 us
    unnamed x41, local copies, waits for them, and re-layouts  18.6 us
    convert_element_type x4, other arithmetic, attend_head(): probs_low = probs.astype(jnp.bfloat16)  15.5 us
    all_to_all x1, waiting for transfers between devices, fetch_blocks(): lax.all_to_all(own_values, 'ctx', split_axis=0, concat_axis=0, tiled=True)  14.3 us
  transfers between devices with their start and end apart: 10, of which 9 were waited for; matrix products, arithmetic and copies ran while one was open for 18% of the time, Pallas kernels for 0%

profile of v1, /device:TPU:0, one launch (start us, length us, event | category | flops | bytes accessed | tf_op | source)
XLA Modules:
  0.0 372.9 jit_solution(11197950703657526468)
XLA Ops:
  7.2 8.4 %all-to-all-start = ((bf16[512,4,128]{2,1,0:T(4,128)(2,1)}), bf16[512,4,128]{2,1,0:T(4,128)(2,1)S(1)}, u32[]{:S(2)}, u32[]{:S(2)}) async-start(bf16[512,4,128]{2,1,0:T(4,128)(2,1)} %param.9), calls=%async_computation | async-start | bytes 1048576 | tf_op jit(solution)/shard_map/all_to_all | solution.py:17
  16.3 14.3 %all-to-all-done = bf16[512,4,128]{2,1,0:T(4,128)(2,1)S(1)} async-done(((bf16[512,4,128]{2,1,0:T(4,128)(2,1)}), bf16[512,4,128]{2,1,0:T(4,128)(2,1)S(1)}, u32[]{:S(2)}, u32[]{:S(2)}) %all-to-all-start) | async-done | bytes 524320 | tf_op jit(solution)/shard_map/all_to_all | solution.py:17
  30.6 3.9 %all-to-all-start.2 = ((bf16[512,4,128]{2,1,0:T(4,128)(2,1)}), bf16[512,4,128]{2,1,0:T(4,128)(2,1)S(1)}, u32[]{:S(2)}, u32[]{:S(2)}) async-start(bf16[512,4,128]{2,1,0:T(4,128)(2,1)} %param.8), calls=%async_computation.2 | async-start | bytes 1048576 | tf_op jit(solution)/shard_map/all_to_all | solution.py:16
  49.0 3.9 %all-to-all-start.1 = ((bf16[16,2,1,32,4,128]{5,3,4,1,2,0:T(8,128)(2,1)}), bf16[16,2,1,32,4,128]{5,3,4,1,2,0:T(8,128)(2,1)S(1)}, u32[]{:S(2)}, u32[]{:S(2)}) async-start(bf16[16,2,1,32,4,128]{5,3,4,1,2,0:T(8,128)(2,1)} %fusion.62), calls=%async_computation.1 | async-start | bytes 2097152 | tf_op jit(solution)/shard_map/all_to_all | solution.py:10
  54.8 21.7 %all-to-all-done.1 = bf16[16,2,1,32,4,128]{5,3,4,1,2,0:T(8,128)(2,1)S(1)} async-done(((bf16[16,2,1,32,4,128]{5,3,4,1,2,0:T(8,128)(2,1)}), bf16[16,2,1,32,4,128]{5,3,4,1,2,0:T(8,128)(2,1)S(1)}, u32[]{:S(2)}, u32[]{:S(2)}) %all-to-all-start.1) | async-done | bytes 1048608 | tf_op jit(solution)/shard_map/all_to_all | solution.py:10
  76.5 5.9 %all-to-all-start.3 = ((bf16[2,16,32,4,128]{4,2,3,0,1:T(8,128)(2,1)}), bf16[2,16,32,4,128]{4,2,3,0,1:T(8,128)(2,1)S(1)}, u32[]{:S(2)}, u32[]{:S(2)}) async-start(bf16[2,16,32,4,128]{4,2,3,0,1:T(8,128)(2,1)} %copy.235), calls=%async_computation.3 | async-start | bytes 2097152 | tf_op jit(solution)/shard_map/all_to_all | solution.py:25
  94.4 11.0 %all-to-all-done.3 = bf16[2,16,32,4,128]{4,2,3,0,1:T(8,128)(2,1)S(1)} async-done(((bf16[2,16,32,4,128]{4,2,3,0,1:T(8,128)(2,1)}), bf16[2,16,32,4,128]{4,2,3,0,1:T(8,128)(2,1)S(1)}, u32[]{:S(2)}, u32[]{:S(2)}) %all-to-all-start.3) | async-done | bytes 1048608 | tf_op jit(solution)/shard_map/all_to_all | solution.py:25
  108.9 74.9 %while.19 = (s32[]{:T(128)}, bf16[512,2,4,128]{0,3,1,2:T(8,128)(2,1)}, bf16[512,2,4,128]{0,3,1,2:T(8,128)(2,1)}, f32[1536,4,128]{2,0,1:T(8,128)}, f32[1536,4,128...) while((s32[]{:T(128)}, ...), condition=%wide.region_4.5_spmd, body=%wide.region_0.4_spmd.sunk | while | flops 2434007552 | bytes 79718664 | solution.py:148
  108.9 6.1 %fusion.123 = (f32[2,512]{1,0:T(2,128)S(1)}, f32[2,512,1536]{1,2,0:T(8,128)}) fusion(pred[512,1536]{0,1:T(8,128)(4,1)S(1)} %get-tuple-element.393, bf16[1536,4,128]{2,0,1:T(8,128)(2,1)} %get-tuple-element.394, s32[]{:T(128)} %get-tuple-element.376, bf16[512,2,4,128]{3,0,1,2:T(8,128)(2,1)} %get-tuple-element.395), kind=kOutput, calls=%fused_computation.110.clone.1 | convolution fusion | flops 408946176 | bytes 7738368 | tf_op jit(solution)/shard_map/while/body/eval_jaxpr/sub | solution.py:81
  115.0 3.9 %fusion.124 = bf16[2,512,1536]{1,2,0:T(8,128)(2,1)S(1)} fusion(f32[2,512,1536]{1,2,0:T(8,128)} %get-tuple-element.361, f32[2,512]{1,0:T(2,128)S(1)} %get-tuple-element.362), kind=kLoop, calls=%fused_computation.14.clone.1 | loop fusion | flops 3145728 | bytes 9441280 | tf_op jit(solution)/shard_map/while/body/eval_jaxpr/convert_element_type | solution.py:83
  127.7 6.1 %fusion.123 = (f32[2,512]{1,0:T(2,128)S(1)}, f32[2,512,1536]{1,2,0:T(8,128)}) fusion(pred[512,1536]{0,1:T(8,128)(4,1)S(1)} %get-tuple-element.393, bf16[1536,4,128]{2,0,1:T(8,128)(2,1)} %get-tuple-element.394, s32[]{:T(128)} %get-tuple-element.376, bf16[512,2,4,128]{3,0,1,2:T(8,128)(2,1)} %get-tuple-element.395), kind=kOutput, calls=%fused_computation.110.clone.1 | convolution fusion | flops 408946176 | bytes 7738368 | tf_op jit(solution)/shard_map/while/body/eval_jaxpr/sub | solution.py:81
  146.4 6.1 %fusion.123 = (f32[2,512]{1,0:T(2,128)S(1)}, f32[2,512,1536]{1,2,0:T(8,128)}) fusion(pred[512,1536]{0,1:T(8,128)(4,1)S(1)} %get-tuple-element.393, bf16[1536,4,128]{2,0,1:T(8,128)(2,1)} %get-tuple-element.394, s32[]{:T(128)} %get-tuple-element.376, bf16[512,2,4,128]{3,0,1,2:T(8,128)(2,1)} %get-tuple-element.395), kind=kOutput, calls=%fused_computation.110.clone.1 | convolution fusion | flops 408946176 | bytes 7738368 | tf_op jit(solution)/shard_map/while/body/eval_jaxpr/sub | solution.py:81
  165.1 6.1 %fusion.123 = (f32[2,512]{1,0:T(2,128)S(1)}, f32[2,512,1536]{1,2,0:T(8,128)}) fusion(pred[512,1536]{0,1:T(8,128)(4,1)S(1)} %get-tuple-element.393, bf16[1536,4,128]{2,0,1:T(8,128)(2,1)} %get-tuple-element.394, s32[]{:T(128)} %get-tuple-element.376, bf16[512,2,4,128]{3,0,1,2:T(8,128)(2,1)} %get-tuple-element.395), kind=kOutput, calls=%fused_computation.110.clone.1 | convolution fusion | flops 408946176 | bytes 7738368 | tf_op jit(solution)/shard_map/while/body/eval_jaxpr/sub | solution.py:81
  188.7 6.0 %all-to-all-start.6 = ((f32[2,16,32,4,128]{4,3,2,0,1:T(4,128)}), f32[2,16,32,4,128]{4,3,2,0,1:T(4,128)S(1)}, u32[]{:S(2)}, u32[]{:S(2)}) async-start(f32[2,16,32,4,128]{4,3,2,0,1:T(4,128)} %copy.247), calls=%async_computation.7 | async-start | bytes 4194304 | tf_op jit(solution)/shard_map/all_to_all | solution.py:45
  199.6 36.9 %all-to-all-done.6 = f32[2,16,32,4,128]{4,3,2,0,1:T(4,128)S(1)} async-done(((f32[2,16,32,4,128]{4,3,2,0,1:T(4,128)}), f32[2,16,32,4,128]{4,3,2,0,1:T(4,128)S(1)}, u32[]{:S(2)}, u32[]{:S(2)}) %all-to-all-start.6) | async-done | bytes 2097184 | tf_op jit(solution)/shard_map/all_to_all | solution.py:45
  237.9 9.8 %all-to-all-start.4 = ((f32[2,16,32,4,128]{4,3,2,0,1:T(4,128)}), f32[2,16,32,4,128]{4,3,2,0,1:T(4,128)S(1)}, u32[]{:S(2)}, u32[]{:S(2)}) async-start(f32[2,16,32,4,128]{4,3,2,0,1:T(4,128)} %copy.242), calls=%async_computation.4 | async-start | bytes 4194304 | tf_op jit(solution)/shard_map/all_to_all | solution.py:38
  247.6 3.9 %reshape.96 = f32[2,16,16384]{2,0,1:T(2,128)} reshape(f32[2,16,32,4,128]{4,3,2,0,1:T(4,128)} %copy-done) | data formatting | bytes 4194304 | tf_op jit(solution)/shard_map/reshape | solution.py:59
  251.5 4.2 %copy.300 = f32[2,16,16384]{2,1,0:T(8,128)} copy(f32[2,16,16384]{2,0,1:T(2,128)} %reshape.96) | data formatting | bytes 4194304 | tf_op jit(solution)/shard_map/reshape | solution.py:59
  264.3 25.9 %all-to-all-done.4 = f32[2,16,32,4,128]{4,3,2,0,1:T(4,128)S(1)} async-done(((f32[2,16,32,4,128]{4,3,2,0,1:T(4,128)}), f32[2,16,32,4,128]{4,3,2,0,1:T(4,128)S(1)}, u32[]{:S(2)}, u32[]{:S(2)}) %all-to-all-start.4) | async-done | bytes 2097184 | tf_op jit(solution)/shard_map/all_to_all | solution.py:38
  290.2 9.8 %all-to-all-start.7 = ((f32[16,32,4,128]{3,2,1,0:T(4,128)}), f32[16,32,4,128]{3,2,1,0:T(4,128)S(1)}, u32[]{:S(2)}, u32[]{:S(2)}) async-start(f32[16,32,4,128]{3,2,1,0:T(4,128)} %copy.250), calls=%async_computation.8 | async-start | bytes 2097152 | tf_op jit(solution)/shard_map/all_to_all | solution.py:65
  312.8 10.8 %all-to-all-done.7 = f32[16,32,4,128]{3,2,1,0:T(4,128)S(1)} async-done(((f32[16,32,4,128]{3,2,1,0:T(4,128)}), f32[16,32,4,128]{3,2,1,0:T(4,128)S(1)}, u32[]{:S(2)}, u32[]{:S(2)}) %all-to-all-start.7) | async-done | bytes 1048608 | tf_op jit(solution)/shard_map/all_to_all | solution.py:65
  323.7 5.9 %all-to-all-start.5 = ((f32[16,32,4,128]{3,2,1,0:T(4,128)}), f32[16,32,4,128]{3,2,1,0:T(4,128)S(1)}, u32[]{:S(2)}, u32[]{:S(2)}) async-start(f32[16,32,4,128]{3,2,1,0:T(4,128)} %copy.245), calls=%async_computation.5 | async-start | bytes 2097152 | tf_op jit(solution)/shard_map/all_to_all | solution.py:64
  332.2 20.3 %all-to-all-done.5 = f32[16,32,4,128]{3,2,1,0:T(4,128)S(1)} async-done(((f32[16,32,4,128]{3,2,1,0:T(4,128)}), f32[16,32,4,128]{3,2,1,0:T(4,128)S(1)}, u32[]{:S(2)}, u32[]{:S(2)}) %all-to-all-start.5) | async-done | bytes 1048608 | tf_op jit(solution)/shard_map/all_to_all | solution.py:64
  360.1 3.9 %reduce-scatter.3.cloned.1.call-done = f32[512,2,128]{2,0,1:T(8,128)} async-done(((f32[512,4,128]{2,0,1:T(8,128)}), f32[512,2,128]{2,0,1:T(8,128)}) %reduce-scatter.3.cloned.1.call-update) | async-done | bytes 524304 | tf_op jit(solution)/shard_map/reduce_scatter | solution.py:151
  (171 shorter events, 122.1 us)
Async XLA Ops:
  7.2 23.4 %all-to-all-start = ((bf16[512,4,128]{2,1,0:T(4,128)(2,1)}), bf16[512,4,128]{2,1,0:T(4,128)(2,1)S(1)}, u32[]{:S(2)}, u32[]{:S(2)}) async-start(bf16[512,4,128]{2,1,0:T(4,128)(2,1)} %param.9), calls=%async_computation | async-start | bytes 1048576 | tf_op jit(solution)/shard_map/all_to_all | solution.py:17
  30.6 18.4 %all-to-all-start.2 = ((bf16[512,4,128]{2,1,0:T(4,128)(2,1)}), bf16[512,4,128]{2,1,0:T(4,128)(2,1)S(1)}, u32[]{:S(2)}, u32[]{:S(2)}) async-start(bf16[512,4,128]{2,1,0:T(4,128)(2,1)} %param.8), calls=%async_computation.2 | async-start | bytes 1048576 | tf_op jit(solution)/shard_map/all_to_all | solution.py:16
  49.0 27.5 %all-to-all-start.1 = ((bf16[16,2,1,32,4,128]{5,3,4,1,2,0:T(8,128)(2,1)}), bf16[16,2,1,32,4,128]{5,3,4,1,2,0:T(8,128)(2,1)S(1)}, u32[]{:S(2)}, u32[]{:S(2)}) async-start(bf16[16,2,1,32,4,128]{5,3,4,1,2,0:T(8,128)(2,1)} %fusion.62), calls=%async_computation.1 | async-start | bytes 2097152 | tf_op jit(solution)/shard_map/all_to_all | solution.py:10
  53.0 29.4 %copy-start.3 = (bf16[512,4,128]{2,1,0:T(4,128)(2,1)S(1)}, bf16[512,4,128]{2,1,0:T(4,128)(2,1)}, u32[]{:S(2)}) copy-start(bf16[512,4,128]{2,1,0:T(4,128)(2,1)} %param.9) | copy-start | bytes 1572868
  53.8 29.5 %copy-start.4 = (bf16[512,4,128]{2,1,0:T(4,128)(2,1)S(1)}, bf16[512,4,128]{2,1,0:T(4,128)(2,1)}, u32[]{:S(2)}) copy-start(bf16[512,4,128]{2,1,0:T(4,128)(2,1)} %param.8) | copy-start | bytes 1572868
  53.8 30.4 %copy-start.12 = (s32[16,2]{0,1:T(2,128)S(1)}, s32[16,2]{0,1:T(2,128)}, u32[]{:S(2)}) copy-start(s32[16,2]{0,1:T(2,128)} %param.11) | copy-start | bytes 388
  76.5 28.8 %all-to-all-start.3 = ((bf16[2,16,32,4,128]{4,2,3,0,1:T(8,128)(2,1)}), bf16[2,16,32,4,128]{4,2,3,0,1:T(8,128)(2,1)S(1)}, u32[]{:S(2)}, u32[]{:S(2)}) async-start(bf16[2,16,32,4,128]{4,2,3,0,1:T(8,128)(2,1)} %copy.235), calls=%async_computation.3 | async-start | bytes 2097152 | tf_op jit(solution)/shard_map/all_to_all | solution.py:25
  115.0 4.6 %slice-start = ((s8[6291456]{0:T(1024)(128)(4,1)}), s8[4194304]{0:T(1024)(128)(4,1)S(1)}, s32[]{:S(2)}) async-start(s8[6291456]{0:T(1024)(128)(4,1)} %bitcast.265), calls=%async_computation.12 | async-start | bytes 8388608 | tf_op jit(solution)/shard_map/while
  115.0 3.9 %copy-start.5 = (bf16[512,2,4,128]{0,3,1,2:T(8,128)(2,1)S(1)}, bf16[512,2,4,128]{0,3,1,2:T(8,128)(2,1)}, u32[]{:S(2)}) copy-start(bf16[512,2,4,128]{0,3,1,2:T(8,128)(2,1)} %get-tuple-element.377) | copy-start | bytes 3145732 | tf_op jit(solution)/shard_map/while
  115.0 5.0 %slice-start.1 = ((s8[6291456]{0:T(1024)(128)(4,1)}), s8[2097152]{0:T(1024)(128)(4,1)S(1)}, s32[]{:S(2)}) async-start(s8[6291456]{0:T(1024)(128)(4,1)} %bitcast.265), calls=%async_computation.13 | async-start | bytes 4194304 | tf_op jit(solution)/shard_map/while
  133.8 4.6 %slice-start = ((s8[6291456]{0:T(1024)(128)(4,1)}), s8[4194304]{0:T(1024)(128)(4,1)S(1)}, s32[]{:S(2)}) async-start(s8[6291456]{0:T(1024)(128)(4,1)} %bitcast.265), calls=%async_computation.12 | async-start | bytes 8388608 | tf_op jit(solution)/shard_map/while
  133.8 5.0 %slice-start.1 = ((s8[6291456]{0:T(1024)(128)(4,1)}), s8[2097152]{0:T(1024)(128)(4,1)S(1)}, s32[]{:S(2)}) async-start(s8[6291456]{0:T(1024)(128)(4,1)} %bitcast.265), calls=%async_computation.13 | async-start | bytes 4194304 | tf_op jit(solution)/shard_map/while
  152.5 4.6 %slice-start = ((s8[6291456]{0:T(1024)(128)(4,1)}), s8[4194304]{0:T(1024)(128)(4,1)S(1)}, s32[]{:S(2)}) async-start(s8[6291456]{0:T(1024)(128)(4,1)} %bitcast.265), calls=%async_computation.12 | async-start | bytes 8388608 | tf_op jit(solution)/shard_map/while
  152.5 5.0 %slice-start.1 = ((s8[6291456]{0:T(1024)(128)(4,1)}), s8[2097152]{0:T(1024)(128)(4,1)S(1)}, s32[]{:S(2)}) async-start(s8[6291456]{0:T(1024)(128)(4,1)} %bitcast.265), calls=%async_computation.13 | async-start | bytes 4194304 | tf_op jit(solution)/shard_map/while
  171.2 4.6 %slice-start = ((s8[6291456]{0:T(1024)(128)(4,1)}), s8[4194304]{0:T(1024)(128)(4,1)S(1)}, s32[]{:S(2)}) async-start(s8[6291456]{0:T(1024)(128)(4,1)} %bitcast.265), calls=%async_computation.12 | async-start | bytes 8388608 | tf_op jit(solution)/shard_map/while
  171.3 5.0 %slice-start.1 = ((s8[6291456]{0:T(1024)(128)(4,1)}), s8[2097152]{0:T(1024)(128)(4,1)S(1)}, s32[]{:S(2)}) async-start(s8[6291456]{0:T(1024)(128)(4,1)} %bitcast.265), calls=%async_computation.13 | async-start | bytes 4194304 | tf_op jit(solution)/shard_map/while
  188.7 47.8 %all-to-all-start.6 = ((f32[2,16,32,4,128]{4,3,2,0,1:T(4,128)}), f32[2,16,32,4,128]{4,3,2,0,1:T(4,128)S(1)}, u32[]{:S(2)}, u32[]{:S(2)}) async-start(f32[2,16,32,4,128]{4,3,2,0,1:T(4,128)} %copy.247), calls=%async_computation.7 | async-start | bytes 4194304 | tf_op jit(solution)/shard_map/all_to_all | solution.py:45
  237.9 52.3 %all-to-all-start.4 = ((f32[2,16,32,4,128]{4,3,2,0,1:T(4,128)}), f32[2,16,32,4,128]{4,3,2,0,1:T(4,128)S(1)}, u32[]{:S(2)}, u32[]{:S(2)}) async-start(f32[2,16,32,4,128]{4,3,2,0,1:T(4,128)} %copy.242), calls=%async_computation.4 | async-start | bytes 4194304 | tf_op jit(solution)/shard_map/all_to_all | solution.py:38
  290.2 33.5 %all-to-all-start.7 = ((f32[16,32,4,128]{3,2,1,0:T(4,128)}), f32[16,32,4,128]{3,2,1,0:T(4,128)S(1)}, u32[]{:S(2)}, u32[]{:S(2)}) async-start(f32[16,32,4,128]{3,2,1,0:T(4,128)} %copy.250), calls=%async_computation.8 | async-start | bytes 2097152 | tf_op jit(solution)/shard_map/all_to_all | solution.py:65
  323.7 28.8 %all-to-all-start.5 = ((f32[16,32,4,128]{3,2,1,0:T(4,128)}), f32[16,32,4,128]{3,2,1,0:T(4,128)S(1)}, u32[]{:S(2)}, u32[]{:S(2)}) async-start(f32[16,32,4,128]{3,2,1,0:T(4,128)} %copy.245), calls=%async_computation.5 | async-start | bytes 2097152 | tf_op jit(solution)/shard_map/all_to_all | solution.py:64
  329.5 28.5 %reduce-scatter.5.cloned.1.call-start = ((), (), s32[]{:S(2)}) async-start(), calls=%async_computation.11 | async-start | bytes 1572864 | tf_op jit(solution)/shard_map/reduce_scatter | solution.py:152
  332.1 23.0 %copy-start.7 = (bf16[512,2,4,128]{0,3,1,2:T(8,128)(2,1)S(1)}, bf16[512,2,4,128]{0,3,1,2:T(8,128)(2,1)}, u32[]{:S(2)}) copy-start(bf16[512,2,4,128]{0,3,1,2:T(8,128)(2,1)} %get-tuple-element.260) | copy-start | bytes 3145732
  332.1 31.9 %reduce-scatter.3.cloned.1.call-start = ((), (), s32[]{:S(2)}) async-start(), calls=%async_computation.10 | async-start | bytes 1572864 | tf_op jit(solution)/shard_map/reduce_scatter | solution.py:151
  352.6 4.0 %copy-start.10 = (bf16[512,2,4,128]{0,3,1,2:T(8,128)(2,1)S(1)}, bf16[512,2,4,128]{0,3,1,2:T(8,128)(2,1)}, u32[]{:S(2)}) copy-start(bf16[512,2,4,128]{0,3,1,2:T(8,128)(2,1)} %get-tuple-element.261) | copy-start | bytes 3145732
  (19 other events, 43.6 us)
Sparse Core Ops, SparseCore 0:
  332.6 9.6 reduce-scatter.4
  355.2 8.7 reduce-scatter.2
